TPU v7x, 128 devices: a whole 4x4x4 slice. The times are simulated.
128 devices in a mesh: dp: 4 (over z), context: 4 (over y), tensor: 8 (over x, core).
Axes of the slice: x: 4, y: 4, z: 4, core: 2. Of those that a mesh axis runs over, the one named last changes fastest.
Arguments:
- inputs: bfloat16 [8192, 5376], P(('dp', 'context')), may hold values from -8 to 8
- queries: bfloat16 [8192, 2048], P(('dp', 'context'), 'tensor'), may hold values from -8 to 8
- key_states: bfloat16 [8192, 1024], P(('dp', 'context'), 'tensor'), may hold values from -8 to 8
- value_states: bfloat16 [8192, 1024], P(('dp', 'context'), 'tensor'), may hold values from -6 to 6
- out_grad: bfloat16 [8192, 5376], P(('dp', 'context')), may hold values from -8 to 8
- positions: int32 [8192], P(('dp', 'context')), may hold values from 0 to 10239, as said below
- w_query: bfloat16 [5376, 2048], P(None, 'tensor'), may hold values from -0.078125 to 0.078125
- w_key: bfloat16 [5376, 1024], P(None, 'tensor'), may hold values from -0.078125 to 0.078125
- w_value: bfloat16 [5376, 1024], P(None, 'tensor'), may hold values from -0.078125 to 0.078125
- w_output: bfloat16 [5376, 2048], P(None, 'tensor'), may hold values from -0.125 to 0.125
Outputs:
- input_grad: bfloat16 [8192, 5376], P(('dp', 'context', 'tensor'))
- grad_query: float32 [5376, 2048], P(('dp', 'context'), 'tensor')
- grad_key: float32 [5376, 1024], P(('dp', 'context'), 'tensor')
- grad_value: float32 [5376, 1024], P(('dp', 'context'), 'tensor')
- grad_output: float32 [5376, 2048], P(('dp', 'context'), 'tensor')
Inputs may be any that keep to these rules, and one draw needn't show every extreme that they name: Within a document positions rise by one from token to token; a position of 0 starts a new document; the first document of each replica's 2048 tokens may have begun before them.
All inputs are finite; a program needn't handle non-finite values.
Results may differ from a plain program's by a relative error of at most 0.02.
Values may be sent and summed in bfloat16 or wider, within the bound.
A program may use at most 128 MiB of HBM per device.

v0:
```python
import jax
import jax.numpy as jnp
from jax import lax
from jax.sharding import PartitionSpec as P

HD = 128
W = 1024
QSCALAR = 168


def rotate_back(grads, places):
    count = grads.shape[0]
    half = HD // 2
    index = jnp.arange(half, dtype=jnp.float32)
    freq = jnp.power(jnp.float32(10000.0), index * (-2.0 / HD))
    angle = places.astype(jnp.float32)[:, None] * freq[None, :]
    cosine = jnp.cos(angle)[:, None, :]
    sine = jnp.sin(angle)[:, None, :]
    split = grads.reshape(count, -1, 2, half)
    first = split[:, :, 0, :]
    second = split[:, :, 1, :]
    upper = first * cosine + second * sine
    lower = second * cosine - first * sine
    return jnp.stack([upper, lower], axis=2).reshape(count, -1)


def contract_rows(left, right):
    return lax.dot_general(
        left, right, (((0,), (0,)), ((), ())), preferred_element_type=jnp.float32
    )


def contract_cols(left, right):
    return lax.dot_general(
        left, right, (((1,), (1,)), ((), ())), preferred_element_type=jnp.float32
    )


def on_device(
    inputs,
    queries,
    key_states,
    value_states,
    out_grad,
    positions,
    w_query,
    w_key,
    w_value,
    w_output,
):
    count = queries.shape[0]
    head_cols = queries.shape[1]
    kv_cols = key_states.shape[1]
    kv_here = kv_cols // HD
    group = head_cols // kv_cols
    scale = QSCALAR ** (-0.5)
    block = lax.axis_index("context")
    blocks = lax.axis_size("context")
    reach = min((W + count - 2) // count, blocks - 1)
    span = (reach + 1) * count
    whole_keys, whole_values = (
        lax.all_gather(key_states, "context", axis=0, tiled=True),
        lax.all_gather(value_states, "context", axis=0, tiled=True),
    )
    padding = jnp.zeros((reach * count, kv_cols), jnp.bfloat16)
    band_keys = lax.dynamic_slice_in_dim(
        jnp.concatenate([padding, whole_keys], axis=0), block * count, span, 0
    )
    band_values = lax.dynamic_slice_in_dim(
        jnp.concatenate([padding, whole_values], axis=0), block * count, span, 0
    )
    query_index = block * count + jnp.arange(count, dtype=jnp.int32)
    key_index = (block - reach) * count + jnp.arange(span, dtype=jnp.int32)
    doc_start = query_index - positions
    allowed = (key_index[None, :] <= query_index[:, None]) & (
        query_index[:, None] - key_index[None, :] < W
    )
    allowed = allowed & (key_index[None, :] >= doc_start[:, None]) & (key_index[None, :] >= 0)
    query_heads = queries.reshape(count, kv_here, group, HD)
    key_heads = band_keys.reshape(span, kv_here, HD)
    value_heads = band_values.reshape(span, kv_here, HD)
    scores = (
        jnp.einsum("qhgd,khd->hgqk", query_heads, key_heads, preferred_element_type=jnp.float32)
        * scale
    )
    scores = jnp.where(allowed, scores, -1e30)
    top = jnp.max(scores, axis=-1, keepdims=True)
    weights = jnp.exp(scores - top)
    probs = weights / jnp.sum(weights, axis=-1, keepdims=True)
    probs_half = probs.astype(jnp.bfloat16)
    attn = jnp.einsum(
        "hgqk,khd->qhgd", probs_half, value_heads, preferred_element_type=jnp.float32
    ).astype(jnp.bfloat16)
    attn_flat = attn.reshape(count, head_cols)
    dattn = jnp.dot(out_grad, w_output, preferred_element_type=jnp.float32).astype(jnp.bfloat16)
    dattn_heads = dattn.reshape(count, kv_here, group, HD)
    dprobs = jnp.einsum(
        "qhgd,khd->hgqk", dattn_heads, value_heads, preferred_element_type=jnp.float32
    )
    delta = jnp.sum(dattn_heads.astype(jnp.float32) * attn.astype(jnp.float32), axis=-1)
    delta = jnp.transpose(delta, (1, 2, 0))[..., None]
    dscores = (probs * (dprobs - delta) * scale).astype(jnp.bfloat16)
    query_grad = jnp.einsum(
        "hgqk,khd->qhgd", dscores, key_heads, preferred_element_type=jnp.float32
    ).reshape(count, head_cols)
    band_key_grad = jnp.einsum(
        "hgqk,qhgd->khd", dscores, query_heads, preferred_element_type=jnp.float32
    ).reshape(span, kv_cols)
    band_value_grad = jnp.einsum(
        "hgqk,qhgd->khd", probs_half, dattn_heads, preferred_element_type=jnp.float32
    ).reshape(span, kv_cols)
    seg_len = blocks * count
    empty = jnp.zeros((seg_len + reach * count, kv_cols), jnp.float32)
    full_keys = lax.dynamic_update_slice_in_dim(empty, band_key_grad, block * count, 0)[
        reach * count :
    ]
    full_values = lax.dynamic_update_slice_in_dim(empty, band_value_grad, block * count, 0)[
        reach * count :
    ]
    key_grad, value_grad = (
        lax.psum_scatter(full_keys, "context", scatter_dimension=0, tiled=True),
        lax.psum_scatter(full_values, "context", scatter_dimension=0, tiled=True),
    )
    query_lin = rotate_back(query_grad, positions).astype(jnp.bfloat16)
    key_lin = rotate_back(key_grad, positions).astype(jnp.bfloat16)
    value_half = value_grad.astype(jnp.bfloat16)
    total = contract_cols(query_lin, w_query)
    total = total + contract_cols(key_lin, w_key)
    total = total + contract_cols(value_half, w_value)
    input_grad = lax.psum_scatter(total, "tensor", scatter_dimension=0, tiled=True).astype(
        jnp.bfloat16
    )
    terms = (
        contract_rows(inputs, query_lin),
        contract_rows(inputs, key_lin),
        contract_rows(inputs, value_half),
        contract_rows(out_grad, attn_flat),
    )
    summed = (
        lax.psum_scatter(
            terms[0].astype(jnp.bfloat16), ("dp", "context"), scatter_dimension=0, tiled=True
        ).astype(jnp.float32),
        lax.psum_scatter(
            terms[1].astype(jnp.bfloat16), ("dp", "context"), scatter_dimension=0, tiled=True
        ).astype(jnp.float32),
        lax.psum_scatter(
            terms[2].astype(jnp.bfloat16), ("dp", "context"), scatter_dimension=0, tiled=True
        ).astype(jnp.float32),
        lax.psum_scatter(
            terms[3].astype(jnp.bfloat16), ("dp", "context"), scatter_dimension=0, tiled=True
        ).astype(jnp.float32),
    )
    return (input_grad, summed[0], summed[1], summed[2], summed[3])


def solution(mesh):
    return jax.shard_map(
        on_device,
        mesh=mesh,
        in_specs=(
            P(("dp", "context"), None),
            P(("dp", "context"), "tensor"),
            P(("dp", "context"), "tensor"),
            P(("dp", "context"), "tensor"),
            P(("dp", "context"), None),
            P(("dp", "context")),
            P(None, "tensor"),
            P(None, "tensor"),
            P(None, "tensor"),
            P(None, "tensor"),
        ),
        out_specs=(
            P(("dp", "context", "tensor"), None),
            P(("dp", "context"), "tensor"),
            P(("dp", "context"), "tensor"),
            P(("dp", "context"), "tensor"),
            P(("dp", "context"), "tensor"),
        ),
        check_vma=False,
    )
```

profile of v0, /device:TPU:1, one launch (start us, length us, event | category | flops | bytes accessed | tf_op | source)
XLA Modules:
  0.0 441.3 jit_solution(8427026727097141793)
XLA Ops:
  7.3 0.6 iota_add_fusion.1
  7.8 1.4 fusion.64
  9.3 13.3 %all_gather.6 = bf16[2048,128]{1,0:T(8,128)(2,1)} all-gather(bf16[512,128]{1,0:T(8,128)(2,1)} %param.12), channel_id=1, replica_groups=mesh['dp'=4,'context'=4,'tensor'=8] {'context'}, dimensions={0}, use_global_device_ids=true | all-gather | bytes 655360 | tf_op jit(solution)/shard_map/all_gather | solution.py:62
  22.6 10.8 %all_gather.7 = bf16[2048,128]{1,0:T(8,128)(2,1)} all-gather(bf16[512,128]{1,0:T(8,128)(2,1)} %param.13), channel_id=1, replica_groups=mesh['dp'=4,'context'=4,'tensor'=8] {'context'}, dimensions={0}, use_global_device_ids=true | all-gather | bytes 655360 | tf_op jit(solution)/shard_map/all_gather | solution.py:63
  33.4 2.3 fusion.17
  35.7 2.5 fusion.9
  38.3 1.5 fusion.8
  39.8 2.3 copy-done.8
  42.1 1.6 convolution_convert_fusion.4
  43.7 3.1 fusion.29
  46.8 3.2 fusion.10
  50.1 0.1 broadcast_in_dim.10.clone.1
  50.2 1.5 copy-done.1
  51.8 1.2 fusion.25
  53.0 1.1 slice.26
  54.1 0.1 broadcast_in_dim.10.clone
  54.2 4.2 fusion.22
  58.4 1.1 slice.29
  59.5 0.2 all-reduce.7.cloned.1.call-start
  59.8 23.1 %reduce-scatter.12.cloned.1.call-done = f32[512,128]{0,1:T(8,128)} async-done(((f32[2048,128]{0,1:T(8,128)}), f32[512,128]{0,1:T(8,128)}) %reduce-scatter.12.cloned.1.call-update) | async-done | bytes 262160 | tf_op jit(solution)/shard_map/reduce_scatter | solution.py:121
  82.9 1.5 fusion.47
  84.4 4.6 %fusion.2 = bf16[5376,128]{0,1:T(8,128)(2,1)} fusion(bf16[512,128]{0,1:T(8,128)(2,1)S(1)} %bitcast.146, bf16[512,5376]{1,0:T(8,128)(2,1)} %param.10), kind=kOutput, calls=%fused_computation.7 | convolution fusion | flops 705331200 | bytes 7012352 | tf_op jit(solution)/shard_map/dot_general | solution.py:28
  89.0 19.8 %reduce-scatter.14.cloned.1.call-done = f32[512,128]{0,1:T(8,128)} async-done(((f32[2048,128]{0,1:T(8,128)}), f32[512,128]{0,1:T(8,128)}) %reduce-scatter.14.cloned.1.call-update) | async-done | bytes 262160 | tf_op jit(solution)/shard_map/reduce_scatter | solution.py:122
  108.8 4.6 %fusion.3 = bf16[5376,128]{0,1:T(8,128)(2,1)} fusion(bf16[512,5376]{1,0:T(8,128)(2,1)} %param.10, f32[512,128]{0,1:T(8,128)} %reduce-scatter.14.cloned.1.call-done), kind=kOutput, calls=%fused_computation.8 | convolution fusion | flops 705396736 | bytes 7143424 | tf_op jit(solution)/shard_map/dot_general | solution.py:28
  113.5 0.5 multiply_cosine_fusion.1
  114.1 2.8 fusion.36
  117.0 5.7 %fusion = bf16[5376,256]{0,1:T(8,128)(2,1)} fusion(bf16[512,256]{0,1:T(8,128)(2,1)S(1)} %bitcast.148, bf16[512,5376]{1,0:T(8,128)(2,1)} %param.10), kind=kOutput, calls=%fused_computation.3 | convolution fusion | flops 1410662400 | bytes 8519680 | tf_op jit(solution)/shard_map/dot_general | solution.py:28
  122.7 4.8 %copy.64 = bf16[5376,256]{1,0:T(8,128)(2,1)} copy(bf16[5376,256]{0,1:T(8,128)(2,1)} %fusion) | data formatting | bytes 5505024
  127.7 5.8 %fusion.1 = bf16[5376,256]{0,1:T(8,128)(2,1)} fusion(bf16[512,256]{0,1:T(8,128)(2,1)S(1)} %bitcast.153, bf16[512,5376]{1,0:T(8,128)(2,1)} %param.14), kind=kOutput, calls=%fused_computation.4 | convolution fusion | flops 1410662400 | bytes 8519680 | tf_op jit(solution)/shard_map/dot_general | solution.py:28
  133.5 4.7 %copy.70 = bf16[5376,256]{1,0:T(8,128)(2,1)} copy(bf16[5376,256]{0,1:T(8,128)(2,1)} %fusion.1) | data formatting | bytes 5505024
  138.2 0.3 reduce-scatter.16.cloned.1.call-start
  138.5 3.1 fusion.65
  141.6 5.8 %fusion.51 = f32[512,5376]{1,0:T(8,128)} fusion(bf16[5376,128]{1,0:T(8,128)(2,1)S(1)} %copy-done.4, f32[512,128]{0,1:T(8,128)S(1)} %copy-done.5), kind=kOutput, calls=%fused_computation.65 | convolution fusion | flops 704708608 | bytes 12648448 | tf_op jit(solution)/shard_map/dot_general | solution.py:34
  147.4 10.0 %add_add_fusion = f32[512,5376]{1,0:T(8,128)} fusion(f32[512,5376]{1,0:T(8,128)} %fusion.51, f32[512,5376]{1,0:T(8,128)S(1)} %fusion.65, bf16[512,256]{0,1:T(8,128)(2,1)S(1)} %bitcast.149, bf16[5376,256]{1,0:T(8,128)(2,1)S(1)} %copy-done), kind=kOutput, calls=%fused_computation | convolution fusion | flops 1414791168 | bytes 36044800 | tf_op jit(solution)/shard_map/dot_general | solution.py:34
  157.4 0.6 copy-done.11
  158.1 0.6 dynamic-slice
  159.3 49.0 %all-reduce.7.cloned.1.call-done = (bf16[5376,128]{0,1:T(8,128)(2,1)}, bf16[5376,128]{0,1:T(8,128)(2,1)}) async-done(((bf16[5376,128]{0,1:T(8,128)(2,1)}, bf16[5376,128]{0,1:T(8,128)(2,1)}), (bf16[5376,128]{0,1:T(8,128)(2,1)}, bf16[5376,128]{0,1:T(8,128)(2,1)})) %all-reduce.7.cloned.1.call-update) | async-done | bytes 2752528
  208.3 1.1 dynamic-slice_convert_fusion
  209.4 0.8 copy.51
  210.2 0.8 copy.52
  211.0 74.9 %reduce-scatter.18.cloned.1.call-done = bf16[336,256]{1,0:T(8,128)(2,1)} async-done(((bf16[5376,256]{1,0:T(8,128)(2,1)}), bf16[336,256]{1,0:T(8,128)(2,1)}) %reduce-scatter.18.cloned.1.call-update) | async-done | bytes 172048
  285.9 1.1 copy.65
  287.0 0.9 copy.50
  287.8 76.9 %reduce-scatter.20.cloned.1.call-done = bf16[336,256]{1,0:T(8,128)(2,1)} async-done(((bf16[5376,256]{1,0:T(8,128)(2,1)}), bf16[336,256]{1,0:T(8,128)(2,1)}) %reduce-scatter.20.cloned.1.call-update) | async-done | bytes 172048
  364.7 1.1 copy.71
  365.8 0.9 copy.53
  366.7 65.5 %reduce-scatter.16.cloned.1.call-done = f32[64,5376]{1,0:T(8,128)} async-done(((f32[512,5376]{1,0:T(8,128)}), f32[64,5376]{1,0:T(8,128)}) %reduce-scatter.16.cloned.1.call-update) | async-done | bytes 1376272 | tf_op jit(solution)/shard_map/reduce_scatter | solution.py:130
  432.2 2.3 convert_element_type.102
  (42 shorter events, 0.5 us)
Async XLA Ops:
  7.2 140.2 %copy-start = (bf16[5376,256]{1,0:T(8,128)(2,1)S(1)}, bf16[5376,256]{1,0:T(8,128)(2,1)}, u32[]{:S(2)}) copy-start(bf16[5376,256]{1,0:T(8,128)(2,1)} %param.16) | copy-start | bytes 8257540
  7.2 75.7 %reduce-scatter.12.cloned.1.call-start = ((), (), s32[]{:S(2)}) async-start(), calls=%async_computation.5 | async-start | bytes 1310720 | tf_op jit(solution)/shard_map/reduce_scatter | solution.py:121
  33.4 6.3 %slice-start = ((s8[5505024]{0:T(1024)(128)(4,1)}), s8[4194304]{0:T(1024)(128)(4,1)S(1)}, s32[]{:S(2)}) async-start(s8[5505024]{0:T(1024)(128)(4,1)} %bitcast.151), calls=%async_computation.11 | async-start | bytes 8388608
  35.7 4.1 slice-start.1
  38.2 8.6 %copy-start.2 = (f32[1536,512,2]{1,0,2:T(8,128)}, f32[1536,512,2]{1,0,2:T(8,128)S(1)}, u32[]{:S(2)}) copy-start(f32[1536,512,2]{1,0,2:T(8,128)S(1)} %get-tuple-element.31) | copy-start | bytes 18874372
  38.2 3.8 copy-start.8
  42.1 1.6 copy-start.6
  43.7 3.1 copy-start.10
  46.8 4.9 %copy-start.7 = (bf16[512,256]{1,0:T(8,128)(2,1)S(1)}, bf16[512,256]{1,0:T(8,128)(2,1)}, u32[]{:S(2)}) copy-start(bf16[512,256]{1,0:T(8,128)(2,1)} %param.11) | copy-start | bytes 786436
  50.1 1.7 copy-start.1
  54.0 54.8 %reduce-scatter.14.cloned.1.call-start = ((), (), s32[]{:S(2)}) async-start(), calls=%async_computation.6 | async-start | bytes 1310720 | tf_op jit(solution)/shard_map/reduce_scatter | solution.py:122
  59.5 148.8 %all-reduce.7.cloned.1.call-start = ((), (), s32[]{:S(2)}) async-start(), calls=%async_computation.10 | async-start | bytes 5505024
  89.0 25.1 %copy-start.3 = (bf16[2048,128]{1,0:T(8,128)(2,1)S(1)}, bf16[2048,128]{1,0:T(8,128)(2,1)}, u32[]{:S(2)}) copy-start(bf16[2048,128]{1,0:T(8,128)(2,1)} %all_gather.6) | copy-start | bytes 1572868
  113.5 172.4 %reduce-scatter.18.cloned.1.call-start = ((), (), s32[]{:S(2)}) async-start(), calls=%async_computation.8 | async-start | bytes 2924544
  122.7 4.9 %copy-start.9 = (bf16[128,2,512]{2,0,1:T(8,128)(2,1)S(1)}, bf16[128,2,512]{2,0,1:T(8,128)(2,1)}, u32[]{:S(2)}) copy-start(bf16[128,2,512]{2,0,1:T(8,128)(2,1)} %get-tuple-element.33) | copy-start | bytes 786436
  127.6 237.1 %reduce-scatter.20.cloned.1.call-start = ((), (), s32[]{:S(2)}) async-start(), calls=%async_computation.9 | async-start | bytes 2924544
  138.2 3.4 copy-start.5
  138.2 294.0 %reduce-scatter.16.cloned.1.call-start = ((), (), s32[]{:S(2)}) async-start(), calls=%async_computation.7 | async-start | bytes 12386304 | tf_op jit(solution)/shard_map/reduce_scatter | solution.py:130
  138.5 3.1 copy-start.4
  157.4 0.7 copy-start.11
Sparse Core Ops, SparseCore 0:
  54.2 28.6 reduce-scatter.11
  85.3 23.5 reduce-scatter.13
  113.6 94.6 all-reduce.6
  211.5 74.3 reduce-scatter.17
  289.1 75.6 reduce-scatter.19
  367.0 65.1 reduce-scatter.15
where the time goes:
time: 442 us; the launch traced here: 441 us
  waiting for transfers between devices  309 us (70%)
  matrix products  58.3 us (13%)
  blocking collectives  24.1 us (5%)
  local copies, waits for them, and re-layouts  22.5 us (5%)
  between operations  15 us (3%)
  other arithmetic  11.3 us (3%)
    unnamed x9, waiting for transfers between devices  201 us
    reduce_scatter x1, waiting for transfers between devices, on_device(): lax.psum_scatter(total, 'tensor', scatter_dimension=0, tiled=True)  65.5 us
    reduce_scatter x1, waiting for transfers between devices, on_device(): lax.psum_scatter(full_keys, 'context', scatter_dimension=0, tiled=True)  23.1 us
    dot_general x4, matrix products, contract_rows(): lax.dot_general(left, right, (((0,), (0,)), ((), ())), preferred_element_...  20.8 us
    unnamed x37, local copies, waits for them, and re-layouts  20.1 us
    reduce_scatter x1, waiting for transfers between devices, on_device(): lax.psum_scatter(full_values, 'context', scatter_dimension=0, tiled=True)  19.8 us
    dot_general x3, matrix products, contract_cols(): lax.dot_general(left, right, (((1,), (1,)), ((), ())), preferred_element_...  18.9 us
    all_gather x1, blocking collectives, on_device(): lax.all_gather(key_states, 'context', axis=0, tiled=True)  13.3 us
  transfers between devices with their start and end apart: 6, of which 6 were waited for; matrix products, arithmetic and copies ran while one was open for 14% of the time, Pallas kernels for 0%

commit v1 on v0

--- a/solution.py
+++ b/solution.py
@@ -6,6 +6,15 @@
 HD = 128
 W = 1024
 QSCALAR = 168
+cut_spot_in = lambda incoming_x, comm_axis: jnp.concatenate(
+    lax.all_to_all(
+        jnp.stack([incoming_x for _ in range(lax.axis_size(comm_axis))], axis=0),
+        axis_name=comm_axis,
+        split_axis=0,
+        concat_axis=0,
+    ),
+    axis=0,
+)
 
 
 def rotate_back(grads, places):
@@ -59,7 +68,7 @@
     reach = min((W + count - 2) // count, blocks - 1)
     span = (reach + 1) * count
     whole_keys, whole_values = (
-        lax.all_gather(key_states, "context", axis=0, tiled=True),
+        cut_spot_in(key_states, comm_axis="context"),
         lax.all_gather(value_states, "context", axis=0, tiled=True),
     )
     padding = jnp.zeros((reach * count, kv_cols), jnp.bfloat16)

time: 442 us -> 437 us (0.989)
  blocking collectives: 24.1 us -> 13.5 us
  starting transfers between devices: 0.65 us -> 5.61 us
    all_gather x1 -> x0, blocking collectives: 13.3 us -> none  [on_device(): lax.all_gather(key_states, 'context', axis=0, tiled=True)]
    all_to_all x0 -> x1, starting transfers between devices: none -> 5 us  [lax.all_to_all(jnp.stack([incoming_x for _ in range(lax.axis_size(comm_ax...]
    unnamed x37 -> x33, local copies, waits for them, and re-layouts: 20.1 us -> 18 us
  transfers between devices with their start and end apart: 6 -> 7, of which waited for: 6 -> 6; matrix products, arithmetic and copies ran while one was open for 14% -> 16% of each run, Pallas kernels for 0% -> 0%
where the time goes in v1:
time: 437 us; the launch traced here: 436 us
  waiting for transfers between devices  307 us (70%)
  matrix products  62 us (14%)
  local copies, waits for them, and re-layouts  22.3 us (5%)
  between operations  15 us (3%)
  blocking collectives  13.5 us (3%)
  other arithmetic  10.4 us (2%)
  starting transfers between devices  5.61 us (1%)
    unnamed x9, waiting for transfers between devices  201 us
    reduce_scatter x1, waiting for transfers between devices, on_device(): lax.psum_scatter(total, 'tensor', scatter_dimension=0, tiled=True)  65.5 us
    reduce_scatter x1, waiting for transfers between devices, on_device(): lax.psum_scatter(full_keys, 'context', scatter_dimension=0, tiled=True)  20.9 us
    dot_general x4, matrix products, contract_rows(): lax.dot_general(left, right, (((0,), (0,)), ((), ())), preferred_element_...  20.7 us
    reduce_scatter x1, waiting for transfers between devices, on_device(): lax.psum_scatter(full_values, 'context', scatter_dimension=0, tiled=True)  19.8 us
    dot_general x3, matrix products, contract_cols(): lax.dot_general(left, right, (((1,), (1,)), ((), ())), preferred_element_...  18.9 us
    unnamed x33, local copies, waits for them, and re-layouts  18 us
    all_gather x1, blocking collectives, on_device(): lax.all_gather(value_states, 'context', axis=0, tiled=True)  13.5 us
  transfers between devices with their start and end apart: 7, of which 6 were waited for; matrix products, arithmetic and copies ran while one was open for 16% of the time, Pallas kernels for 0%

profile of v1, /device:TPU:1, one launch (start us, length us, event | category | flops | bytes accessed | tf_op | source)
XLA Modules:
  0.0 436.2 jit_solution(15270053207200182407)
XLA Ops:
  7.2 1.9 stack.8
  9.1 5.0 %all-to-all-start = ((bf16[4,512,128]{2,1,0:T(8,128)(2,1)}), bf16[4,512,128]{2,1,0:T(8,128)(2,1)}, u32[]{:S(2)}, u32[]{:S(2)}) async-start(bf16[4,512,128]{2,1,0:T(8,128)(2,1)} %stack.8), calls=%async_computation | async-start | bytes 1048576 | tf_op jit(solution)/shard_map/all_to_all | solution.py:10
  14.1 0.6 iota_add_fusion.1
  14.7 1.3 fusion.64
  16.0 13.5 %all_gather.3 = bf16[2048,128]{1,0:T(8,128)(2,1)} all-gather(bf16[512,128]{1,0:T(8,128)(2,1)} %param.13), channel_id=1, replica_groups=mesh['dp'=4,'context'=4,'tensor'=8] {'context'}, dimensions={0}, use_global_device_ids=true | all-gather | bytes 655360 | tf_op jit(solution)/shard_map/all_gather | solution.py:72
  29.6 5.8 %convolution_convert_fusion.4 = bf16[512,256]{0,1:T(8,128)(2,1)} fusion(bf16[512,5376]{1,0:T(8,128)(2,1)} %param.14, bf16[5376,256]{1,0:T(8,128)(2,1)} %param.19), kind=kOutput, calls=%fused_computation.33 | convolution fusion | flops 1409417216 | bytes 8519680 | tf_op jit(solution)/shard_map/dot_general | solution.py:104
  35.4 1.4 fusion.17
  36.8 2.5 fusion.9
  39.3 1.5 fusion.8
  40.8 0.2 copy-done.10
  40.9 3.1 fusion.29
  44.0 3.2 fusion.10
  47.2 0.1 broadcast_in_dim.10.clone.1
  47.3 1.6 copy-done.1
  48.9 1.2 fusion.25
  50.0 1.0 slice.26
  51.3 4.2 fusion.22
  55.5 1.1 slice.29
  56.6 0.2 all-reduce.7.cloned.1.call-start
  56.9 20.9 %reduce-scatter.12.cloned.1.call-done = f32[512,128]{0,1:T(8,128)} async-done(((f32[2048,128]{0,1:T(8,128)}), f32[512,128]{0,1:T(8,128)}) %reduce-scatter.12.cloned.1.call-update) | async-done | bytes 262160 | tf_op jit(solution)/shard_map/reduce_scatter | solution.py:130
  77.8 1.5 fusion.47
  79.3 4.6 %fusion.2 = bf16[5376,128]{0,1:T(8,128)(2,1)} fusion(bf16[512,128]{0,1:T(8,128)(2,1)S(1)} %bitcast.147, bf16[512,5376]{1,0:T(8,128)(2,1)} %param.10), kind=kOutput, calls=%fused_computation.7 | convolution fusion | flops 705331200 | bytes 7012352 | tf_op jit(solution)/shard_map/dot_general | solution.py:37
  83.9 19.8 %reduce-scatter.14.cloned.1.call-done = f32[512,128]{0,1:T(8,128)} async-done(((f32[2048,128]{0,1:T(8,128)}), f32[512,128]{0,1:T(8,128)}) %reduce-scatter.14.cloned.1.call-update) | async-done | bytes 262160 | tf_op jit(solution)/shard_map/reduce_scatter | solution.py:131
  103.7 4.7 %fusion.3 = bf16[5376,128]{0,1:T(8,128)(2,1)} fusion(bf16[512,5376]{1,0:T(8,128)(2,1)} %param.10, f32[512,128]{0,1:T(8,128)} %reduce-scatter.14.cloned.1.call-done), kind=kOutput, calls=%fused_computation.8 | convolution fusion | flops 705396736 | bytes 7143424 | tf_op jit(solution)/shard_map/dot_general | solution.py:37
  108.4 0.5 multiply_cosine_fusion.1
  109.0 2.6 fusion.36
  111.7 5.7 %fusion = bf16[5376,256]{0,1:T(8,128)(2,1)} fusion(bf16[512,256]{0,1:T(8,128)(2,1)S(1)} %bitcast.149, bf16[512,5376]{1,0:T(8,128)(2,1)} %param.10), kind=kOutput, calls=%fused_computation.3 | convolution fusion | flops 1410662400 | bytes 8519680 | tf_op jit(solution)/shard_map/dot_general | solution.py:37
  117.4 4.9 %copy.64 = bf16[5376,256]{1,0:T(8,128)(2,1)} copy(bf16[5376,256]{0,1:T(8,128)(2,1)} %fusion) | data formatting | bytes 5505024
  122.4 5.8 %fusion.1 = bf16[5376,256]{0,1:T(8,128)(2,1)} fusion(bf16[512,256]{0,1:T(8,128)(2,1)S(1)} %bitcast.152, bf16[512,5376]{1,0:T(8,128)(2,1)} %param.14), kind=kOutput, calls=%fused_computation.4 | convolution fusion | flops 1410662400 | bytes 8519680 | tf_op jit(solution)/shard_map/dot_general | solution.py:37
  128.2 4.7 %copy.70 = bf16[5376,256]{1,0:T(8,128)(2,1)} copy(bf16[5376,256]{0,1:T(8,128)(2,1)} %fusion.1) | data formatting | bytes 5505024
  132.9 0.3 reduce-scatter.16.cloned.1.call-start
  133.2 3.1 fusion.65
  136.3 5.8 %fusion.51 = f32[512,5376]{1,0:T(8,128)} fusion(bf16[5376,128]{1,0:T(8,128)(2,1)S(1)} %copy-done.3, f32[512,128]{0,1:T(8,128)S(1)} %copy-done.4), kind=kOutput, calls=%fused_computation.65 | convolution fusion | flops 704708608 | bytes 12648448 | tf_op jit(solution)/shard_map/dot_general | solution.py:43
  142.1 10.0 %add_add_fusion = f32[512,5376]{1,0:T(8,128)} fusion(f32[512,5376]{1,0:T(8,128)} %fusion.51, f32[512,5376]{1,0:T(8,128)S(1)} %fusion.65, bf16[512,256]{0,1:T(8,128)(2,1)S(1)} %bitcast.150, bf16[5376,256]{1,0:T(8,128)(2,1)S(1)} %copy-done), kind=kOutput, calls=%fused_computation | convolution fusion | flops 1414791168 | bytes 36044800 | tf_op jit(solution)/shard_map/dot_general | solution.py:43
  152.2 0.6 copy-done.11
  152.8 0.6 dynamic-slice
  154.0 49.2 %all-reduce.7.cloned.1.call-done = (bf16[5376,128]{0,1:T(8,128)(2,1)}, bf16[5376,128]{0,1:T(8,128)(2,1)}) async-done(((bf16[5376,128]{0,1:T(8,128)(2,1)}, bf16[5376,128]{0,1:T(8,128)(2,1)}), (bf16[5376,128]{0,1:T(8,128)(2,1)}, bf16[5376,128]{0,1:T(8,128)(2,1)})) %all-reduce.7.cloned.1.call-update) | async-done | bytes 2752528
  203.2 1.1 dynamic-slice_convert_fusion
  204.3 0.8 copy.51
  205.1 0.8 copy.52
  205.9 74.9 %reduce-scatter.18.cloned.1.call-done = bf16[336,256]{1,0:T(8,128)(2,1)} async-done(((bf16[5376,256]{1,0:T(8,128)(2,1)}), bf16[336,256]{1,0:T(8,128)(2,1)}) %reduce-scatter.18.cloned.1.call-update) | async-done | bytes 172048
  280.8 1.1 copy.65
  281.9 0.9 copy.50
  282.7 76.9 %reduce-scatter.20.cloned.1.call-done = bf16[336,256]{1,0:T(8,128)(2,1)} async-done(((bf16[5376,256]{1,0:T(8,128)(2,1)}), bf16[336,256]{1,0:T(8,128)(2,1)}) %reduce-scatter.20.cloned.1.call-update) | async-done | bytes 172048
  359.6 1.1 copy.71
  360.7 0.9 copy.53
  361.6 65.5 %reduce-scatter.16.cloned.1.call-done = f32[64,5376]{1,0:T(8,128)} async-done(((f32[512,5376]{1,0:T(8,128)}), f32[64,5376]{1,0:T(8,128)}) %reduce-scatter.16.cloned.1.call-update) | async-done | bytes 1376272 | tf_op jit(solution)/shard_map/reduce_scatter | solution.py:139
  427.1 2.3 convert_element_type.102
  (39 shorter events, 0.6 us)
Async XLA Ops:
  7.2 135.0 %copy-start = (bf16[5376,256]{1,0:T(8,128)(2,1)S(1)}, bf16[5376,256]{1,0:T(8,128)(2,1)}, u32[]{:S(2)}) copy-start(bf16[5376,256]{1,0:T(8,128)(2,1)} %param.16) | copy-start | bytes 8257540
  9.1 27.7 %all-to-all-start = ((bf16[4,512,128]{2,1,0:T(8,128)(2,1)}), bf16[4,512,128]{2,1,0:T(8,128)(2,1)}, u32[]{:S(2)}, u32[]{:S(2)}) async-start(bf16[4,512,128]{2,1,0:T(8,128)(2,1)} %stack.8), calls=%async_computation | async-start | bytes 1048576 | tf_op jit(solution)/shard_map/all_to_all | solution.py:10
  14.1 63.7 %reduce-scatter.12.cloned.1.call-start = ((), (), s32[]{:S(2)}) async-start(), calls=%async_computation.6 | async-start | bytes 1310720 | tf_op jit(solution)/shard_map/reduce_scatter | solution.py:130
  29.6 5.8 %copy-start.7 = (s32[512]{0:T(512)S(1)}, s32[512]{0:T(512)}, u32[]{:S(2)}) copy-start(s32[512]{0:T(512)} %iota_add_fusion.1) | copy-start | bytes 6148
  29.6 5.8 %copy-start.8 = (s32[512]{0:T(512)S(1)}, s32[512]{0:T(512)}, u32[]{:S(2)}) copy-start(s32[512]{0:T(512)} %get-tuple-element.29) | copy-start | bytes 6148
  39.2 4.7 %copy-start.2 = (f32[1536,512,2]{1,0,2:T(8,128)}, f32[1536,512,2]{1,0,2:T(8,128)S(1)}, u32[]{:S(2)}) copy-start(f32[1536,512,2]{1,0,2:T(8,128)S(1)} %get-tuple-element.31) | copy-start | bytes 18874372
  39.3 1.5 copy-start.5
  39.3 1.7 copy-start.10
  44.0 4.9 %copy-start.6 = (bf16[512,256]{1,0:T(8,128)(2,1)S(1)}, bf16[512,256]{1,0:T(8,128)(2,1)}, u32[]{:S(2)}) copy-start(bf16[512,256]{1,0:T(8,128)(2,1)} %param.11) | copy-start | bytes 786436
  47.2 1.7 copy-start.1
  51.1 52.6 %reduce-scatter.14.cloned.1.call-start = ((), (), s32[]{:S(2)}) async-start(), calls=%async_computation.7 | async-start | bytes 1310720 | tf_op jit(solution)/shard_map/reduce_scatter | solution.py:131
  56.6 146.6 %all-reduce.7.cloned.1.call-start = ((), (), s32[]{:S(2)}) async-start(), calls=%async_computation.11 | async-start | bytes 5505024
  108.4 172.4 %reduce-scatter.18.cloned.1.call-start = ((), (), s32[]{:S(2)}) async-start(), calls=%async_computation.9 | async-start | bytes 2924544
  117.4 5.0 %copy-start.9 = (bf16[128,2,512]{2,0,1:T(8,128)(2,1)S(1)}, bf16[128,2,512]{2,0,1:T(8,128)(2,1)}, u32[]{:S(2)}) copy-start(bf16[128,2,512]{2,0,1:T(8,128)(2,1)} %get-tuple-element.33) | copy-start | bytes 786436
  122.3 237.3 %reduce-scatter.20.cloned.1.call-start = ((), (), s32[]{:S(2)}) async-start(), calls=%async_computation.10 | async-start | bytes 2924544
  132.9 3.4 copy-start.4
  132.9 294.2 %reduce-scatter.16.cloned.1.call-start = ((), (), s32[]{:S(2)}) async-start(), calls=%async_computation.8 | async-start | bytes 12386304 | tf_op jit(solution)/shard_map/reduce_scatter | solution.py:139
  133.2 3.1 copy-start.3
  152.1 0.7 copy-start.11
Sparse Core Ops, SparseCore 0:
  51.2 26.5 reduce-scatter.11
  80.2 23.4 reduce-scatter.13
  108.5 94.6 all-reduce.6
  206.4 74.3 reduce-scatter.17
  284.0 75.6 reduce-scatter.19
  361.9 65.1 reduce-scatter.15
